TPU v7x, 32 devices: a whole 2x2x4 slice. The times are simulated.
32 devices in a mesh: row: 8 (over z, x), col: 4 (over y, core).
Axes of the slice: x: 2, y: 2, z: 4, core: 2. Of those that a mesh axis runs over, the one named last changes fastest.
Arguments:
- receptance: bfloat16 [2, 16384, 16384], P(None, 'row', 'col'), may hold values from -4 to 60, as said below
- coupling: int32 [2, 768], replicated, may hold values from 0 to 16383, as said below
Outputs:
- coupled: bfloat16 [2, 16384, 16384], P(None, 'row', 'col')
Inputs may be any that keep to these rules, and one draw needn't show every extreme that they name: `coupling`: row 0 holds 768 distinct body DOFs, all in the first half of the 16384 DOFs; row 1 holds 768 distinct cavity DOFs, all in the second half. `receptance`: the driving-point entry of every body or cavity DOF named in coupling (same response and excitation DOF) has real part 52 or more; every other real or imaginary part lies within -4 to 4.
All inputs are finite; a program needn't handle non-finite values.
Results may differ from a plain program's by a relative error of at most 0.015.
Values may be sent and summed in bfloat16 or wider, within the bound.
A program may use at most 320 MiB of HBM per device.

v0:
```python
import jax
import jax.numpy as jnp
from jax import lax
from jax.sharding import PartitionSpec as P

SWEEPS = 6


def select_rows(matrix, body_dof, cav_dof, offset, extent):
    count = body_dof.shape[0]
    both_dof = jnp.concatenate([body_dof, cav_dof]) - offset
    inside = (both_dof >= 0) & (both_dof < extent)
    clipped = jnp.clip(both_dof, 0, extent - 1)
    picked = jnp.take(matrix, clipped, axis=1).astype(jnp.float32)
    picked = jnp.where(inside[None, :, None], picked, jnp.zeros((), jnp.float32))
    return picked[:, :count, :] - picked[:, count:, :]


def select_columns(matrix, body_dof, cav_dof, offset, extent):
    positions = offset + lax.broadcasted_iota(jnp.int32, (extent, 1), 0)
    table = (positions == body_dof[None, :]).astype(jnp.float32) - (
        positions == cav_dof[None, :]
    ).astype(jnp.float32)
    table = table.astype(matrix.dtype)
    return jnp.einsum(
        "prc,cn->prn",
        matrix,
        table,
        preferred_element_type=jnp.float32,
        precision=lax.Precision.HIGHEST,
    )


def complex_times(mat_real, mat_imag, vec_real, vec_imag):
    hi = lax.Precision.HIGHEST
    out_real = jnp.dot(mat_real, vec_real, precision=hi) - jnp.dot(mat_imag, vec_imag, precision=hi)
    out_imag = jnp.dot(mat_real, vec_imag, precision=hi) + jnp.dot(mat_imag, vec_real, precision=hi)
    return (out_real, out_imag)


def local(receptance, coupling):
    tile_rows = receptance.shape[1]
    tile_cols = receptance.shape[2]
    row_index = lax.axis_index("row")
    col_index = lax.axis_index("col")
    body_dof = coupling[0]
    cav_dof = coupling[1]
    row_terms = select_rows(receptance, body_dof, cav_dof, row_index * tile_rows, tile_rows)
    rhs_local = lax.psum_scatter(
        row_terms.astype(jnp.bfloat16), "row", scatter_dimension=2, tiled=True
    ).astype(jnp.float32)
    solve_cols = rhs_local.shape[2]
    column_terms = select_columns(receptance, body_dof, cav_dof, col_index * tile_cols, tile_cols)
    left_full = lax.psum(column_terms.astype(jnp.bfloat16), "col")
    first_col = col_index * tile_cols + row_index * solve_cols
    inter_terms = select_columns(rhs_local, body_dof, cav_dof, first_col, solve_cols)
    interface = lax.psum(inter_terms, ("row", "col"))
    z_real = interface[0]
    z_imag = interface[1]
    diag_real = jnp.diagonal(z_real)
    diag_imag = jnp.diagonal(z_imag)
    modulus = diag_real * diag_real + diag_imag * diag_imag
    d_real = (diag_real / modulus)[:, None]
    d_imag = (-diag_imag / modulus)[:, None]

    def scale(part_real, part_imag):
        return (d_real * part_real - d_imag * part_imag, d_real * part_imag + d_imag * part_real)

    v_real = rhs_local[0]
    v_imag = rhs_local[1]
    x_real, x_imag = scale(v_real, v_imag)
    for sweep_index in range(SWEEPS):
        p_real, p_imag = complex_times(z_real, z_imag, x_real, x_imag)
        e_real, e_imag = scale(v_real - p_real, v_imag - p_imag)
        x_real = x_real + e_real
        x_imag = x_imag + e_imag
    weights = jnp.stack([x_real, x_imag]).astype(jnp.bfloat16)
    u_real = left_full[0]
    u_imag = left_full[1]
    column_piece = lax.all_gather(weights, "row", axis=2, tiled=True)
    p_real = column_piece[0]
    p_imag = column_piece[1]
    c_real = jnp.dot(u_real, p_real, preferred_element_type=jnp.float32) - jnp.dot(
        u_imag, p_imag, preferred_element_type=jnp.float32
    )
    c_imag = jnp.dot(u_real, p_imag, preferred_element_type=jnp.float32) + jnp.dot(
        u_imag, p_real, preferred_element_type=jnp.float32
    )
    recv_piece = receptance.astype(jnp.float32)
    return (recv_piece - jnp.stack([c_real, c_imag])).astype(jnp.bfloat16)


def solution(mesh):
    in_specs = (P(None, "row", "col"), P())
    out_specs = P(None, "row", "col")
    return jax.shard_map(local, mesh=mesh, in_specs=in_specs, out_specs=out_specs, check_vma=False)
```

profile of v0, /device:TPU:0, one launch (start us, length us, event | category | flops | bytes accessed | tf_op | source)
XLA Modules:
  0.0 973.6 jit_solution(2592334917314808475)
XLA Ops:
  6.5 0.8 slice_reduce_fusion.1
  7.4 93.4 %gather_fusion = bf16[1536,2,4096]{2,0,1:T(8,128)(2,1)} fusion(bf16[2,2048,4096]{2,1,0:T(8,128)(2,1)} %param.2, s32[2048]{0:T(1024)S(1)} %pad_clamp_fusion), kind=kCustom, calls=%fused_computation | custom fusion | bytes 50337792 | tf_op jit(solution)/shard_map/jit(_take)/gather | solution.py:14
  100.8 27.7 %select_bitcast_fusion = f32[2,1536,4096]{2,1,0:T(8,128)} fusion(bf16[1536,2,4096]{2,0,1:T(8,128)(2,1)} %gather_fusion, pred[1536]{0:T(1024)(128)(4,1)S(1)} %get-tuple-element.24, pred[1536]{0:T(1024)(128)(4,1)S(1)} %get-tuple-element.23), kind=kLoop, calls=%fused_computation.5 | loop fusion | flops 37748736 | bytes 75500544 | tf_op jit(solution)/shard_map/jit(_where)/select_n | solution.py:15
  128.5 21.2 %fusion.1 = bf16[2,768,4096]{2,1,0:T(8,128)(2,1)} fusion(f32[2,1536,4096]{2,1,0:T(8,128)} %select_bitcast_fusion), kind=kLoop, calls=%fused_computation.9 | loop fusion | flops 12582912 | bytes 62914560 | tf_op jit(solution)/shard_map/convert_element_type | solution.py:50
  149.7 0.0 all-reduce.5.cloned.1.call-start
  149.8 207.7 %reduce-scatter.2.cloned.1.call-done = bf16[2,768,512]{2,1,0:T(8,128)(2,1)} async-done(((bf16[2,768,4096]{2,1,0:T(8,128)(2,1)}), bf16[2,768,512]{2,1,0:T(8,128)(2,1)}) %reduce-scatter.2.cloned.1.call-update) | async-done | bytes 1572880 | tf_op jit(solution)/shard_map/reduce_scatter | solution.py:49
  357.5 7.8 fusion.24
  365.4 0.0 all-reduce.3.cloned.1.call-start
  365.4 31.4 %convert_bitcast_fusion = bf16[2,2048,768]{1,2,0:T(8,128)(2,1)} fusion(bf16[2,2048,4096]{2,1,0:T(8,128)(2,1)} %param.2, s32[4096]{0:T(1024)S(1)} %iota_add_fusion, s32[768]{0:T(1024)S(1)} %get-tuple-element.6, s32[768]{0:T(1024)S(1)} %get-tuple-element.5), kind=kOutput, calls=%fused_computation.15 | convolution fusion | flops 25791823872 | bytes 39868416 | tf_op jit(solution)/shard_map/prc,cn->prn/dot_general | solution.py:25
  396.8 0.0 all-gather.2.cloned.1.call-start
  396.9 1.3 copy-done.1
  398.2 2.1 convert_element_type.47
  400.3 108.9 %all-reduce.5.cloned.1.call-done = f32[2,768,768]{2,1,0:T(8,128)} async-done(((f32[2,768,768]{2,1,0:T(8,128)}), f32[2,768,768]{2,1,0:T(8,128)}) %all-reduce.5.cloned.1.call-update) | async-done | bytes 4718608 | tf_op jit(solution)/shard_map/psum | solution.py:57
  509.2 4.1 slice_bitcast_fusion.13
  513.4 12.4 %gather_fusion.1 = f32[768]{0:T(1024)S(1)} fusion(f32[768,768]{1,0:T(8,128)} %get-tuple-element.9, s32[768]{0:T(1024)S(1)} %or_reduce_fusion), kind=kCustom, calls=%fused_computation.1 | custom fusion | bytes 12288 | tf_op jit(solution)/shard_map/jit(diagonal)/cond/branch_0_fun/gather | solution.py:60
  525.8 6.5 gather_fusion.2
  532.3 6.9 fusion.12
  539.2 6.9 fusion.14
  546.1 4.3 bitcast_subtract_fusion.11
  550.3 5.1 fusion.21
  555.5 3.9 fusion.58
  559.4 3.9 fusion.57
  563.2 3.9 bitcast_subtract_fusion.10
  567.2 4.8 subtract_add_fusion.3
  572.0 3.9 fusion.56
  575.9 3.9 fusion.55
  579.7 3.9 bitcast_subtract_fusion.9
  583.7 4.5 subtract_add_fusion.2
  588.2 3.9 fusion.54
  592.1 3.9 fusion.53
  596.0 4.2 bitcast_subtract_fusion.8
  600.2 4.3 subtract_add_fusion.1
  604.5 3.9 fusion.52
  608.4 3.9 fusion.51
  612.3 4.4 bitcast_subtract_fusion.7
  616.7 4.3 subtract_add_fusion
  621.0 3.9 fusion.49
  624.9 3.9 fusion.50
  628.8 4.2 bitcast_subtract_fusion
  633.0 4.5 fusion.35
  637.5 1.3 pad_maximum_fusion
  638.8 0.0 all-reduce.3.cloned.1.call-done
  638.8 175.8 %all-gather.2.cloned.1.call-done = bf16[2,768,4096]{2,1,0:T(8,128)(2,1)} async-done(((bf16[2,768,512]{2,1,0:T(8,128)(2,1)}), bf16[2,768,4096]{2,1,0:T(8,128)(2,1)}) %all-gather.2.cloned.1.call-update) | async-done | bytes 12582928 | tf_op jit(solution)/shard_map/all_gather | solution.py:80
  814.6 23.2 %fusion.9 = f32[2048,4096]{1,0:T(8,128)} fusion(bf16[2,768,4096]{2,1,0:T(8,128)(2,1)} %all-gather.2.cloned.1.call-done, bf16[2,2048,768]{1,2,0:T(8,128)(2,1)} %all-reduce.3.cloned.1.call-done), kind=kOutput, calls=%fused_computation.20 | convolution fusion | flops 12884901888 | bytes 42991616 | tf_op jit(solution)/shard_map/dot_general | solution.py:86
  837.8 20.2 %fusion.8 = f32[2048,4096]{1,0:T(8,128)} fusion(bf16[2,768,4096]{2,1,0:T(8,128)(2,1)} %all-gather.2.cloned.1.call-done, bf16[2,2048,768]{1,2,0:T(8,128)(2,1)S(1)} %copy-done.2), kind=kOutput, calls=%fused_computation.19 | convolution fusion | flops 12884901888 | bytes 42991616 | tf_op jit(solution)/shard_map/dot_general | solution.py:83
  858.1 33.0 %add_bitcast_fusion = f32[1,2048,4096]{2,1,0:T(8,128)} fusion(f32[2048,4096]{1,0:T(8,128)} %fusion.9, bf16[2,768,4096]{2,1,0:T(8,128)(2,1)} %all-gather.2.cloned.1.call-done, bf16[2,2048,768]{1,2,0:T(8,128)(2,1)} %all-reduce.3.cloned.1.call-done), kind=kOutput, calls=%fused_computation.6 | convolution fusion | flops 12893290496 | bytes 76546048 | tf_op jit(solution)/shard_map/dot_general | solution.py:86
  891.0 33.3 %subtract_bitcast_fusion = f32[1,2048,4096]{2,1,0:T(8,128)} fusion(f32[2048,4096]{1,0:T(8,128)} %fusion.8, bf16[2,768,4096]{2,1,0:T(8,128)(2,1)} %all-gather.2.cloned.1.call-done, bf16[2,2048,768]{1,2,0:T(8,128)(2,1)} %all-reduce.3.cloned.1.call-done), kind=kOutput, calls=%fused_computation.7 | convolution fusion | flops 12893290496 | bytes 76546048 | tf_op jit(solution)/shard_map/dot_general | solution.py:83
  924.3 42.3 %fusion = bf16[2,2048,4096]{2,1,0:T(8,128)(2,1)} fusion(f32[1,2048,4096]{2,1,0:T(8,128)} %add_bitcast_fusion, f32[1,2048,4096]{2,1,0:T(8,128)} %subtract_bitcast_fusion, bf16[2,2048,4096]{2,1,0:T(8,128)(2,1)} %param.2), kind=kLoop, calls=%fused_computation.4 | loop fusion | flops 67108864 | bytes 134217728 | tf_op jit(solution)/shard_map/convert_element_type | solution.py:90
  (22 shorter events, 0.2 us)
Async XLA Ops:
  6.5 351.0 %reduce-scatter.2.cloned.1.call-start = ((), (), s32[]{:S(2)}) async-start(), calls=%async_computation.2 | async-start | bytes 14155776 | tf_op jit(solution)/shard_map/reduce_scatter | solution.py:49
  149.7 359.5 %all-reduce.5.cloned.1.call-start = ((), (), s32[]{:S(2)}) async-start(), calls=%async_computation.3 | async-start | bytes 9437184 | tf_op jit(solution)/shard_map/psum | solution.py:57
  365.4 273.4 %all-reduce.3.cloned.1.call-start = ((), (), s32[]{:S(2)}) async-start(), calls=%async_computation.1 | async-start | bytes 12582912 | tf_op jit(solution)/shard_map/psum | solution.py:54
  396.8 1.4 copy-start.1
  396.8 417.8 %all-gather.2.cloned.1.call-start = ((), (), s32[]{:S(2)}) async-start(), calls=%async_computation.4 | async-start | bytes 14155776 | tf_op jit(solution)/shard_map/all_gather | solution.py:80
  525.7 20.3 %slice-start = ((s8[4718592]{0:T(1024)(128)(4,1)}), s8[524288]{0:T(1024)(128)(4,1)S(1)}, s32[]{:S(2)}) async-start(s8[4718592]{0:T(1024)(128)(4,1)} %bitcast.150), calls=%async_computation.5 | async-start | bytes 1048576
  532.3 13.8 %slice-start.1 = ((s8[4718592]{0:T(1024)(128)(4,1)}), s8[4194304]{0:T(1024)(128)(4,1)S(1)}, s32[]{:S(2)}) async-start(s8[4718592]{0:T(1024)(128)(4,1)} %bitcast.150), calls=%async_computation.6 | async-start | bytes 8388608
  539.2 6.9 copy-start
  814.6 23.2 %copy-start.2 = (bf16[2,2048,768]{1,2,0:T(8,128)(2,1)S(1)}, bf16[2,2048,768]{1,2,0:T(8,128)(2,1)}, u32[]{:S(2)}) copy-start(bf16[2,2048,768]{1,2,0:T(8,128)(2,1)} %all-reduce.3.cloned.1.call-done) | copy-start | bytes 18874372
Sparse Core Ops, SparseCore 0:
  149.8 207.6 reduce-scatter.1
  365.5 143.7 all-reduce.4
  511.8 118.4 all-reduce.2
  638.9 175.7 all-gather.1
where the time goes:
time: 984 us; the launch traced here: 974 us
  waiting for transfers between devices  493 us (50%)
  matrix products  254 us (26%)
  local copies, waits for them, and re-layouts  119 us (12%)
  other arithmetic  94.7 us (10%)
  between operations  13.9 us (1%)
    reduce_scatter x1, waiting for transfers between devices, local(): lax.psum_scatter(row_terms.astype(jnp.bfloat16), 'row', scatter_dimension...  208 us
    all_gather x1, waiting for transfers between devices, local(): column_piece = lax.all_gather(weights, 'row', axis=2, tiled=True)  176 us
    psum x1, waiting for transfers between devices, local(): interface = lax.psum(inter_terms, ('row', 'col'))  109 us
    gather x1, local copies, waits for them, and re-layouts, select_rows(): picked = jnp.take(matrix, clipped, axis=1).astype(jnp.float32)  93.4 us
    convert_element_type x1, other arithmetic, local(): return (recv_piece - jnp.stack([c_real, c_imag])).astype(jnp.bfloat16)  42.3 us
    dot_general x2, matrix products, select_columns(): jnp.einsum('prc,cn->prn', matrix, table, preferred_element_type=jnp.float...  39.2 us
    dot_general x1, matrix products, local(): jnp.dot(u_imag, p_imag, preferred_element_type=jnp.float32)  33.3 us
    dot_general x1, matrix products, local(): jnp.dot(u_imag, p_real, preferred_element_type=jnp.float32)  33 us
  transfers between devices with their start and end apart: 4, of which 3 were waited for; matrix products, arithmetic and copies ran while one was open for 17% of the time, Pallas kernels for 0%

commit v1 on v0

--- a/solution.py
+++ b/solution.py
@@ -4,6 +4,28 @@
 from jax.sharding import PartitionSpec as P
 
 SWEEPS = 6
+
+
+def laid_out(tiles, dim):
+    lengths = list(tiles.shape[1:])
+    lengths[dim] *= tiles.shape[0]
+    return jnp.moveaxis(tiles, 0, dim).reshape(lengths)
+
+
+def gather_around(x, axis, dim):
+    length = lax.axis_size(axis)
+    pairs = [(i, (i + 1) % length) for i in range(length)]
+    back = [(b, a) for a, b in pairs]
+    lower, upper = ([], [])
+    for step in range(length - 1):
+        if step % 2 == 0:
+            lower.append(lax.ppermute(lower[-1] if lower else x, axis, pairs))
+        else:
+            upper.append(lax.ppermute(upper[-1] if upper else x, axis, back))
+    blocks = jnp.stack([*lower[::-1], x, *upper])
+    shift = lax.axis_index(axis) - len(lower)
+    blocks = blocks[(jnp.arange(length) - shift) % length]
+    return laid_out(blocks, dim)
 
 
 def select_rows(matrix, body_dof, cav_dof, offset, extent):
@@ -77,7 +99,7 @@
     weights = jnp.stack([x_real, x_imag]).astype(jnp.bfloat16)
     u_real = left_full[0]
     u_imag = left_full[1]
-    column_piece = lax.all_gather(weights, "row", axis=2, tiled=True)
+    column_piece = gather_around(weights, "row", 2)
     p_real = column_piece[0]
     p_imag = column_piece[1]
     c_real = jnp.dot(u_real, p_real, preferred_element_type=jnp.float32) - jnp.dot(

time: 984 us -> 1140 us (1.16)
  local copies, waits for them, and re-layouts: 119 us -> 175 us
  waiting for transfers between devices: 493 us -> 539 us
  starting transfers between devices: 0.13 us -> 45.7 us
    all_gather x1 -> x0, waiting for transfers between devices: 176 us -> none  [local(): column_piece = lax.all_gather(weights, 'row', axis=2, tiled=True)]
    ppermute x0 -> x7, waiting for transfers between devices: none -> 164 us  [the longest x4 164 us: gather_around(): lower.append(lax.ppermute(lower[-1] if lower else x, axis, pairs))]
    ppermute x0 -> x7, starting transfers between devices: none -> 45.6 us  [the longest x3 39.2 us: gather_around(): upper.append(lax.ppermute(upper[-1] if upper else x, axis, back))]
    psum x1, waiting for transfers between devices: 109 us -> 141 us  [local(): interface = lax.psum(inter_terms, ('row', 'col'))]
    slice x0 -> x3, local copies, waits for them, and re-layouts: none -> 28.2 us  [the longest x2 19.5 us: local(): p_real = column_piece[0]]
    psum x1, waiting for transfers between devices: 0.02 us -> 27.2 us  [local(): left_full = lax.psum(column_terms.astype(jnp.bfloat16), 'col')]
    unnamed x10 -> x22, local copies, waits for them, and re-layouts: 1.35 us -> 17.8 us
  transfers between devices with their start and end apart: 4 -> 10, of which waited for: 3 -> 7; matrix products, arithmetic and copies ran while one was open for 17% -> 8% of each run, Pallas kernels for 0% -> 0%
where the time goes in v1:
time: 1140 us; the launch traced here: 1130 us
  waiting for transfers between devices  539 us (47%)
  matrix products  256 us (22%)
  local copies, waits for them, and re-layouts  175 us (15%)
  other arithmetic  94.8 us (8%)
  starting transfers between devices  45.7 us (4%)
  between operations  15.6 us (1%)
    reduce_scatter x1, waiting for transfers between devices, local(): lax.psum_scatter(row_terms.astype(jnp.bfloat16), 'row', scatter_dimension...  208 us
    ppermute x4, waiting for transfers between devices, gather_around(): lower.append(lax.ppermute(lower[-1] if lower else x, axis, pairs))  164 us
    psum x1, waiting for transfers between devices, local(): interface = lax.psum(inter_terms, ('row', 'col'))  141 us
    gather x1, local copies, waits for them, and re-layouts, select_rows(): picked = jnp.take(matrix, clipped, axis=1).astype(jnp.float32)  93.4 us
    convert_element_type x1, other arithmetic, local(): return (recv_piece - jnp.stack([c_real, c_imag])).astype(jnp.bfloat16)  42.3 us
    dot_general x2, matrix products, select_columns(): jnp.einsum('prc,cn->prn', matrix, table, preferred_element_type=jnp.float...  39.3 us
    ppermute x3, starting transfers between devices, gather_around(): upper.append(lax.ppermute(upper[-1] if upper else x, axis, back))  39.2 us
    dot_general x1, matrix products, local(): jnp.dot(u_imag, p_imag, preferred_element_type=jnp.float32)  33.3 us
  transfers between devices with their start and end apart: 10, of which 7 were waited for; matrix products, arithmetic and copies ran while one was open for 8% of the time, Pallas kernels for 0%

profile of v1, /device:TPU:0, one launch (start us, length us, event | category | flops | bytes accessed | tf_op | source)
XLA Modules:
  0.0 1126.4 jit_solution(15829516180710175419)
XLA Ops:
  8.2 93.4 %gather_fusion = bf16[1536,2,4096]{2,0,1:T(8,128)(2,1)} fusion(bf16[2,2048,4096]{2,1,0:T(8,128)(2,1)} %param.2, s32[2048]{0:T(1024)S(1)} %pad_clamp_fusion), kind=kCustom, calls=%fused_computation | custom fusion | bytes 50337792 | tf_op jit(solution)/shard_map/jit(_take)/gather | solution.py:36
  101.7 27.7 %select_bitcast_fusion = f32[2,1536,4096]{2,1,0:T(8,128)} fusion(bf16[1536,2,4096]{2,0,1:T(8,128)(2,1)} %gather_fusion, pred[1536]{0:T(1024)(128)(4,1)S(1)} %get-tuple-element.26, pred[1536]{0:T(1024)(128)(4,1)S(1)} %get-tuple-element.25), kind=kLoop, calls=%fused_computation.6 | loop fusion | flops 37748736 | bytes 75500544 | tf_op jit(solution)/shard_map/jit(_where)/select_n | solution.py:37
  129.4 21.2 %fusion.1 = bf16[2,768,4096]{2,1,0:T(8,128)(2,1)} fusion(f32[2,1536,4096]{2,1,0:T(8,128)} %select_bitcast_fusion), kind=kLoop, calls=%fused_computation.10 | loop fusion | flops 12582912 | bytes 62914560 | tf_op jit(solution)/shard_map/convert_element_type | solution.py:72
  150.6 207.7 %reduce-scatter.2.cloned.1.call-done = bf16[2,768,512]{2,1,0:T(8,128)(2,1)} async-done(((bf16[2,768,4096]{2,1,0:T(8,128)(2,1)}), bf16[2,768,512]{2,1,0:T(8,128)(2,1)}) %reduce-scatter.2.cloned.1.call-update) | async-done | bytes 1572880 | tf_op jit(solution)/shard_map/reduce_scatter | solution.py:71
  358.4 7.8 fusion.24
  369.7 140.5 %all-reduce.5.cloned.1.call-done = f32[2,768,768]{2,1,0:T(8,128)} async-done(((f32[2,768,768]{2,1,0:T(8,128)}), f32[2,768,768]{2,1,0:T(8,128)}) %all-reduce.5.cloned.1.call-update) | async-done | bytes 4718608 | tf_op jit(solution)/shard_map/psum | solution.py:79
  510.2 4.1 slice_bitcast_fusion.7
  514.3 12.4 %gather_fusion.1 = f32[768]{0:T(1024)S(1)} fusion(f32[768,768]{1,0:T(8,128)} %get-tuple-element.11, s32[768]{0:T(1024)S(1)} %or_reduce_fusion), kind=kCustom, calls=%fused_computation.1 | custom fusion | bytes 12288 | tf_op jit(solution)/shard_map/jit(diagonal)/cond/branch_0_fun/gather | solution.py:82
  526.8 6.3 gather_fusion.2
  533.1 6.9 fusion.12
  540.0 6.9 fusion.14
  546.9 4.3 bitcast_subtract_fusion.11
  551.1 5.1 fusion.21
  556.2 3.9 fusion.58
  560.1 3.9 fusion.57
  564.0 3.9 bitcast_subtract_fusion.10
  568.0 4.6 subtract_add_fusion.3
  572.5 3.9 fusion.56
  576.4 3.9 fusion.55
  580.3 3.9 bitcast_subtract_fusion.9
  584.3 4.8 subtract_add_fusion.2
  589.0 3.9 fusion.54
  592.9 3.9 fusion.53
  596.8 4.1 bitcast_subtract_fusion.8
  600.9 4.3 subtract_add_fusion.1
  609.2 3.9 fusion.51
  613.1 4.2 bitcast_subtract_fusion.7
  617.2 4.3 subtract_add_fusion
  625.5 3.9 fusion.49
  629.3 4.4 bitcast_subtract_fusion.6
  633.8 4.5 add_convert_fusion.1
  639.7 36.1 %collective-permute-done = bf16[2,768,512]{2,1,0:T(8,128)(2,1)S(1)} collective-permute-done((bf16[2,768,512]{2,1,0:T(8,128)(2,1)S(1)}, bf16[2,768,512]{2,1,0:T(8,128)(2,1)S(1)}, u32[]{:S(2)}, u32[]{:S(2)}) %collective-permute-start) | collective-permute-done | bytes 1572896 | tf_op jit(solution)/shard_map/ppermute | solution.py:22
  677.0 4.7 collective-permute-start.4
  681.7 60.5 %collective-permute-done.1 = bf16[2,768,512]{2,1,0:T(8,128)(2,1)S(1)} collective-permute-done((bf16[2,768,512]{2,1,0:T(8,128)(2,1)S(1)}, bf16[2,768,512]{2,1,0:T(8,128)(2,1)S(1)}, u32[]{:S(2)}, u32[]{:S(2)}) %collective-permute-start.1) | collective-permute-done | bytes 1572896 | tf_op jit(solution)/shard_map/ppermute | solution.py:22
  745.9 32.3 %collective-permute-start.5 = (bf16[2,768,512]{2,1,0:T(8,128)(2,1)}, bf16[2,768,512]{2,1,0:T(8,128)(2,1)}, u32[]{:S(2)}, u32[]{:S(2)}) collective-permute-start(bf16[2,768,512]{2,1,0:T(8,128)(2,1)} %collective-permute-done.4), channel_id=1, source_target_pairs={{4,0},{8,4},{12,8},{16,12},{20,16},{24,20},{28,24},{0,28},{5,1},{9... | collective-permute-start | bytes 4718600 | tf_op jit(solution)/shard_map/ppermute | solution.py:24
  778.2 34.2 %collective-permute-done.2 = bf16[2,768,512]{2,1,0:T(8,128)(2,1)} collective-permute-done((bf16[2,768,512]{2,1,0:T(8,128)(2,1)S(1)}, bf16[2,768,512]{2,1,0:T(8,128)(2,1)}, u32[]{:S(2)}, u32[]{:S(2)}) %collective-permute-start.2) | collective-permute-done | bytes 1572896 | tf_op jit(solution)/shard_map/ppermute | solution.py:22
  815.0 31.4 %convert_bitcast_fusion = bf16[2,2048,768]{1,2,0:T(8,128)(2,1)} fusion(bf16[2,2048,4096]{2,1,0:T(8,128)(2,1)} %param.2, s32[4096]{0:T(1024)S(1)} %iota_add_fusion, s32[768]{0:T(1024)S(1)} %get-tuple-element.6, s32[768]{0:T(1024)S(1)} %get-tuple-element.5), kind=kOutput, calls=%fused_computation.14 | convolution fusion | flops 25791823872 | bytes 39868416 | tf_op jit(solution)/shard_map/prc,cn->prn/dot_general | solution.py:47
  848.7 32.9 %collective-permute-done.3 = bf16[2,768,512]{2,1,0:T(8,128)(2,1)} collective-permute-done((bf16[2,768,512]{2,1,0:T(8,128)(2,1)}, bf16[2,768,512]{2,1,0:T(8,128)(2,1)}, u32[]{:S(2)}, u32[]{:S(2)}) %collective-permute-start.3) | collective-permute-done | bytes 1572896 | tf_op jit(solution)/shard_map/ppermute | solution.py:22
  898.2 11.3 %gather_fusion.3 = bf16[8,2,768,512]{3,2,1,0:T(8,128)(2,1)} fusion(bf16[8,2,768,512]{3,2,1,0:T(8,128)(2,1)} %bitcast_dynamic-update-slice_fusion, s32[1024]{0:T(1024)S(1)} %pad_clamp_fusion.1), kind=kCustom, calls=%fused_computation.3 | custom fusion | bytes 25165856 | tf_op jit(solution)/shard_map/gather | solution.py:27
  909.4 11.0 fusion.59
  920.4 8.5 copy.3
  929.0 8.7 copy.4
  937.6 27.2 %all-reduce.3.cloned.1.call-done = bf16[2,2048,768]{1,2,0:T(8,128)(2,1)} async-done(((bf16[2,2048,768]{1,2,0:T(8,128)(2,1)}), bf16[2,2048,768]{1,2,0:T(8,128)(2,1)}) %all-reduce.3.cloned.1.call-update) | async-done | bytes 6291472 | tf_op jit(solution)/shard_map/psum | solution.py:76
  964.8 22.6 %fusion.10 = f32[2048,4096]{1,0:T(8,128)} fusion(bf16[768,4096]{0,1:T(8,128)(2,1)} %bitcast.170, bf16[2,2048,768]{1,2,0:T(8,128)(2,1)} %all-reduce.3.cloned.1.call-done), kind=kOutput, calls=%fused_computation.20 | convolution fusion | flops 12884901888 | bytes 42991616 | tf_op jit(solution)/shard_map/dot_general | solution.py:108
  987.4 22.4 %fusion.11 = f32[2048,4096]{1,0:T(8,128)} fusion(bf16[768,4096]{0,1:T(8,128)(2,1)} %bitcast.172, bf16[2,2048,768]{1,2,0:T(8,128)(2,1)} %all-reduce.3.cloned.1.call-done), kind=kOutput, calls=%fused_computation.21 | convolution fusion | flops 12884901888 | bytes 42991616 | tf_op jit(solution)/shard_map/dot_general | solution.py:105
  1009.9 33.1 %add_bitcast_fusion = f32[1,2048,4096]{2,1,0:T(8,128)} fusion(f32[2048,4096]{1,0:T(8,128)} %fusion.10, bf16[768,4096]{0,1:T(8,128)(2,1)} %bitcast.173, bf16[2,2048,768]{1,2,0:T(8,128)(2,1)} %all-reduce.3.cloned.1.call-done), kind=kOutput, calls=%fused_computation.7 | convolution fusion | flops 12893290496 | bytes 76546048 | tf_op jit(solution)/shard_map/dot_general | solution.py:108
  1042.9 33.3 %subtract_bitcast_fusion = f32[1,2048,4096]{2,1,0:T(8,128)} fusion(f32[2048,4096]{1,0:T(8,128)} %fusion.11, bf16[768,4096]{0,1:T(8,128)(2,1)} %bitcast.171, bf16[2,2048,768]{1,2,0:T(8,128)(2,1)} %all-reduce.3.cloned.1.call-done), kind=kOutput, calls=%fused_computation.8 | convolution fusion | flops 12893290496 | bytes 76546048 | tf_op jit(solution)/shard_map/dot_general | solution.py:105
  1076.2 42.3 %fusion = bf16[2,2048,4096]{2,1,0:T(8,128)(2,1)} fusion(f32[1,2048,4096]{2,1,0:T(8,128)} %add_bitcast_fusion, f32[1,2048,4096]{2,1,0:T(8,128)} %subtract_bitcast_fusion, bf16[2,2048,4096]{2,1,0:T(8,128)(2,1)} %param.2), kind=kLoop, calls=%fused_computation.5 | loop fusion | flops 67108864 | bytes 134217728 | tf_op jit(solution)/shard_map/convert_element_type | solution.py:112
  (53 shorter events, 39.8 us)
Async XLA Ops:
  7.4 351.0 %reduce-scatter.2.cloned.1.call-start = ((), (), s32[]{:S(2)}) async-start(), calls=%async_computation.2 | async-start | bytes 14155776 | tf_op jit(solution)/shard_map/reduce_scatter | solution.py:71
  150.6 359.6 %all-reduce.5.cloned.1.call-start = ((), (), s32[]{:S(2)}) async-start(), calls=%async_computation.3 | async-start | bytes 9437184 | tf_op jit(solution)/shard_map/psum | solution.py:79
  366.2 1.4 copy-start.5
  366.2 598.6 %all-reduce.3.cloned.1.call-start = ((), (), s32[]{:S(2)}) async-start(), calls=%async_computation.1 | async-start | bytes 12582912 | tf_op jit(solution)/shard_map/psum | solution.py:76
  526.7 20.1 %slice-start = ((s8[4718592]{0:T(1024)(128)(4,1)}), s8[524288]{0:T(1024)(128)(4,1)S(1)}, s32[]{:S(2)}) async-start(s8[4718592]{0:T(1024)(128)(4,1)} %bitcast.163), calls=%async_computation.4 | async-start | bytes 1048576
  533.1 13.8 %slice-start.1 = ((s8[4718592]{0:T(1024)(128)(4,1)}), s8[4194304]{0:T(1024)(128)(4,1)S(1)}, s32[]{:S(2)}) async-start(s8[4718592]{0:T(1024)(128)(4,1)} %bitcast.163), calls=%async_computation.5 | async-start | bytes 8388608
  540.0 6.9 copy-start
  638.4 37.4 %collective-permute-start = (bf16[2,768,512]{2,1,0:T(8,128)(2,1)S(1)}, bf16[2,768,512]{2,1,0:T(8,128)(2,1)S(1)}, u32[]{:S(2)}, u32[]{:S(2)}) collective-permute-start(bf16[2,768,512]{2,1,0:T(8,128)(2,1)S(1)} %pad_maximum_fusion), channel_id=1, source_target_pairs={{0,4},{4,8},{8,12},{12,16},{16,20},{20,24},{24,28},{28,0},{1,5},{5... | collective-permute-start | bytes 4718600 | tf_op jit(solution)/shard_map/ppermute | solution.py:22
  675.8 1.2 copy-start.1
  677.0 65.2 %collective-permute-start.1 = (bf16[2,768,512]{2,1,0:T(8,128)(2,1)S(1)}, bf16[2,768,512]{2,1,0:T(8,128)(2,1)S(1)}, u32[]{:S(2)}, u32[]{:S(2)}) collective-permute-start(bf16[2,768,512]{2,1,0:T(8,128)(2,1)S(1)} %collective-permute-done), channel_id=1, source_target_pairs={{0,4},{4,8},{8,12},{12,16},{16,20},{20,24},{24,28},{28,0},{1,5},{5... | collective-permute-start | bytes 4718600 | tf_op jit(solution)/shard_map/ppermute | solution.py:22
  677.0 68.9 %collective-permute-start.4 = (bf16[2,768,512]{2,1,0:T(8,128)(2,1)S(1)}, bf16[2,768,512]{2,1,0:T(8,128)(2,1)}, u32[]{:S(2)}, u32[]{:S(2)}) collective-permute-start(bf16[2,768,512]{2,1,0:T(8,128)(2,1)S(1)} %pad_maximum_fusion), channel_id=1, source_target_pairs={{4,0},{8,4},{12,8},{16,12},{20,16},{24,20},{28,24},{0,28},{5,1},{9... | collective-permute-start | bytes 4718600 | tf_op jit(solution)/shard_map/ppermute | solution.py:24
  742.2 1.2 copy-start.3
  743.4 69.0 %collective-permute-start.2 = (bf16[2,768,512]{2,1,0:T(8,128)(2,1)S(1)}, bf16[2,768,512]{2,1,0:T(8,128)(2,1)}, u32[]{:S(2)}, u32[]{:S(2)}) collective-permute-start(bf16[2,768,512]{2,1,0:T(8,128)(2,1)S(1)} %collective-permute-done.1), channel_id=1, source_target_pairs={{0,4},{4,8},{8,12},{12,16},{16,20},{20,24},{24,28},{28,0},{1,5},{5... | collective-permute-start | bytes 4718600 | tf_op jit(solution)/shard_map/ppermute | solution.py:22
  745.9 100.6 %collective-permute-start.5 = (bf16[2,768,512]{2,1,0:T(8,128)(2,1)}, bf16[2,768,512]{2,1,0:T(8,128)(2,1)}, u32[]{:S(2)}, u32[]{:S(2)}) collective-permute-start(bf16[2,768,512]{2,1,0:T(8,128)(2,1)} %collective-permute-done.4), channel_id=1, source_target_pairs={{4,0},{8,4},{12,8},{16,12},{20,16},{24,20},{28,24},{0,28},{5,1},{9... | collective-permute-start | bytes 4718600 | tf_op jit(solution)/shard_map/ppermute | solution.py:24
  812.4 69.2 %collective-permute-start.3 = (bf16[2,768,512]{2,1,0:T(8,128)(2,1)}, bf16[2,768,512]{2,1,0:T(8,128)(2,1)}, u32[]{:S(2)}, u32[]{:S(2)}) collective-permute-start(bf16[2,768,512]{2,1,0:T(8,128)(2,1)} %collective-permute-done.2), channel_id=1, source_target_pairs={{0,4},{4,8},{8,12},{12,16},{16,20},{20,24},{24,28},{28,0},{1,5},{5... | collective-permute-start | bytes 4718600 | tf_op jit(solution)/shard_map/ppermute | solution.py:22
  846.5 50.4 %collective-permute-start.6 = (bf16[2,768,512]{2,1,0:T(8,128)(2,1)}, bf16[2,768,512]{2,1,0:T(8,128)(2,1)S(1)}, u32[]{:S(2)}, u32[]{:S(2)}) collective-permute-start(bf16[2,768,512]{2,1,0:T(8,128)(2,1)} %collective-permute-done.5), channel_id=1, source_target_pairs={{4,0},{8,4},{12,8},{16,12},{20,16},{24,20},{28,24},{0,28},{5,1},{9... | collective-permute-start | bytes 4718600 | tf_op jit(solution)/shard_map/ppermute | solution.py:24
  884.2 2.8 copy-start.4
  887.1 2.0 copy-start.2
Sparse Core Ops, SparseCore 0:
  150.7 207.6 reduce-scatter.1
  366.4 143.8 all-reduce.4
Sparse Core Ops, SparseCore 1:
  846.5 118.3 all-reduce.2
